TPU v7x, 32 devices: a whole 2x2x4 slice. The times are simulated.
32 devices in a mesh: grp: 2 (over x), feat: 16 (over z, y, core).
Axes of the slice: x: 2, y: 2, z: 4, core: 2. Of those that a mesh axis runs over, the one named last changes fastest.
Arguments:
- x_acts: bfloat16 [8, 1024, 4096], P('grp'), parts along dimension 0, may hold values from -6 to 6
- delta: bfloat16 [8, 1024, 4096], P('grp', None, 'feat'), parts along dimension 0, may hold values from -6 to 6
- pattern: int32 [32, 32], replicated, may hold values 0 or 1
- row_signs: int32 [4096], replicated, may hold values from -1 to 1, as said below
- col_signs: int32 [4096], replicated, may hold values from -1 to 1, as said below
- cols: int32 [8192], replicated, may hold values from 0 to 16777215
Outputs:
- sketch: float32 [8, 8192], P('grp'), parts along dimension 0
There are 2 independent parts, one for each index of `grp`. A program takes and returns all parts, laid end to end along the dimension named above; an argument that names none is the same for every part. Nothing has to cross between parts.
Inputs may be any that keep to these rules, and one draw needn't show every extreme that they name: `row_signs`: every entry is -1 or +1. `col_signs`: every entry is -1 or +1.
All inputs are finite; a program needn't handle non-finite values.
Results may differ from a plain program's by a relative error of at most 0.0029.
Values may be sent and summed in bfloat16 or wider, within the bound.
No kernel may reach another device: no remote copies, remote signals or barrier semaphores. Data moves between devices by JAX's collectives and lax.ppermute only.
A program may use at most 192 MiB of HBM per device.

v0:
```python
import functools
import math

import jax
import jax.numpy as jnp
from jax import lax
from jax.experimental import pallas as pl
from jax.experimental.pallas import tpu as pltpu
from jax.sharding import PartitionSpec as P

BLK = 128
LANES = 128
SUBLANES = 8
AT_ONCE = 8
GROUP = 4
PARTS = 4
PAD = 8
VMEM_LIMIT = 44 * 2**20


def partner(value, axis, apart):
    mask = 2**apart
    pairs = [(source, source ^ mask) for source in range(lax.axis_size(axis))]
    return lax.ppermute(value, axis, pairs)


def parity(ids):
    for shift in (8, 4, 2, 1):
        ids = ids ^ (ids >> shift)
    return ids & 1


def iota(shape, dim):
    return lax.broadcasted_iota(jnp.int32, shape, dim)


def aligned(index, unit):
    return pl.multiple_of(index * unit, unit)


def butterfly(tiles):
    half = 1
    while half < len(tiles):
        tiles = [
            tiles[q] + tiles[q + half] if q & half == 0 else tiles[q - half] - tiles[q]
            for q in range(len(tiles))
        ]
        half *= 2
    return tiles


def sketch_kernel(
    scale, pattern_hbm, x_hbm, d_hbm, cols_hbm, rows_hbm, signs_hbm, mine_ref, other_ref,
    pattern, cols_ref, rows_ref, signs_ref, small_sem, x_ref, d_ref, dt_ref, had_ref, flip_even, flip_odd, idx_ref, signed_ref, t_ref, x_sem, d_sem, idx_sem, idx_smem, listed,
):
    examples, tokens, width = x_hbm.shape
    rows = d_hbm.shape[2]
    n_cols = width // LANES
    bands = dt_ref.shape[0] // examples
    band = rows // bands
    n_blocks = bands * n_cols
    block_rows = band * examples
    n_kept = cols_ref.shape[0] * LANES
    per_vreg = SUBLANES // examples
    me = lax.axis_index("feat")
    step = tokens // PARTS

    def x_copy(example, part):
        where = pl.ds(part * step, step)
        slot = example % 2
        return pltpu.make_async_copy(
            x_hbm.at[example, where], x_ref.at[slot, where], x_sem.at[slot, part]
        )

    small = [
        pltpu.make_async_copy(source, target, small_sem.at[i])
        for i, (source, target) in enumerate(
            (
                (cols_hbm, cols_ref),
                (pattern_hbm, pattern),
                (rows_hbm, rows_ref),
                (signs_hbm, signs_ref),
            )
        )
    ]
    for copy in small:
        copy.start()
    d_copy = pltpu.make_async_copy(d_hbm, d_ref, d_sem)
    d_copy.start()
    for part in range(PARTS):
        x_copy(0, part).start()

    had_ref[...] = (1 - 2 * parity(iota((band, band), 0) & iota((band, band), 1))).astype(
        jnp.bfloat16
    )
    bits = (iota((SUBLANES, LANES), 1) >> iota((SUBLANES, LANES), 0) & 1).astype(jnp.bfloat16)
    for copy in small:
        copy.wait()

    cols = cols_ref[...]
    kept_row, kept_col = cols // width, cols % width
    local = kept_row % rows
    block = local // band * n_cols + kept_col // LANES
    place = iota(cols.shape, 0) % per_vreg
    idx_ref[...] = PAD + (block * band + local % band) * examples - place * examples

    def flips(group, flip_ref):
        digits = []
        for p in range(per_vreg):
            lane = cols_ref[pl.ds(group * per_vreg + p, 1), :] % LANES
            digits.append((lane >> iota((SUBLANES, LANES), 0) & 1).astype(jnp.bfloat16))
        shared = lax.dot_general(
            jnp.concatenate(digits, axis=1),
            bits,
            (((0,), (0,)), ((), ())),
            preferred_element_type=jnp.float32,
        )
        odd = (shared.astype(jnp.int32) & 1).astype(jnp.float32)
        flip_ref[...] = 1.0 - 2.0 * odd

    first = me * rows // BLK

    count = AT_ONCE
    for b in range(bands):
        for q in range(n_cols):
            listed[count] = b * n_cols + q
            count = count + pattern[first + b, q]
        for extra in range(GROUP):
            listed[count + extra] = n_blocks
        count = (count + GROUP - 1) // GROUP * GROUP
    for extra in range(AT_ONCE):
        listed[count + extra] = n_blocks
    n_steps = jnp.maximum((count - 1) // AT_ONCE, 1)
    for i in range(AT_ONCE):
        listed[i] = listed[n_steps * AT_ONCE + i]

    idx_copy = pltpu.make_async_copy(idx_ref, idx_smem, idx_sem)
    idx_copy.start()

    for b in range(bands):
        def clear(q, carry):
            @pl.when(pattern[first + b, q] == 0)
            def _():
                start = PAD + (b * n_cols + q) * block_rows
                here = pl.ds(pl.multiple_of(start, SUBLANES), block_rows)
                t_ref[here, :] = jnp.zeros((block_rows, LANES), jnp.float32)

            return carry

        lax.fori_loop(0, n_cols, clear, 0)

    if rows % LANES == 0:
        row_flip = jnp.concatenate(
            [rows_ref[pl.ds(me * (rows // LANES) + i, 1), :] for i in range(rows // LANES)],
            axis=1,
        ).astype(jnp.bfloat16)
    else:
        row_flip = rows_ref[...].astype(jnp.bfloat16)
    d_copy.wait()
    for example in range(examples):
        turned = (d_ref[example] * row_flip).T
        for b in range(bands):
            dt_ref[example * bands + b] = turned[b * band : (b + 1) * band, :]

    def finish(at, example):
        sums = jnp.dot(had_ref[...], signed_ref[...], preferred_element_type=jnp.float32)
        for i in range(AT_ONCE):
            start = PAD + listed[at + i] * block_rows + example
            t_ref[pl.ds(start, band, stride=examples), :] = sums[:, i * LANES : (i + 1) * LANES]

    def one_example(example, carry):
        for part in range(PARTS):
            x_copy(example, part).wait()

        @pl.when(example + 1 < examples)
        def _():
            for part in range(PARTS):
                x_copy(example + 1, part).start()


        def some_blocks(s, carry):
            finish(s * AT_ONCE, jnp.where(s == 0, jnp.maximum(example - 1, 0), example))
            for g in range(AT_ONCE // GROUP):
                ids = [listed[(s + 1) * AT_ONCE + g * GROUP + k] for k in range(GROUP)]
                acts = [
                    x_ref[example % 2, :, pl.ds(aligned(i % n_cols, LANES), LANES)] for i in ids
                ]
                flip = [signs_ref[pl.ds(i % n_cols, 1), :] for i in ids]
                grad = jnp.dot(
                    dt_ref[example * bands + ids[0] // n_cols % bands],
                    jnp.concatenate(acts, axis=1),
                    preferred_element_type=jnp.float32,
                )
                flip = jnp.concatenate(flip, axis=1).astype(jnp.float32)
                here = slice(g * GROUP * LANES, (g + 1) * GROUP * LANES)
                signed_ref[:, here] = (grad * flip).astype(jnp.bfloat16)
            return carry

        lax.fori_loop(0, n_steps, some_blocks, 0)

        return carry

    lax.fori_loop(0, examples, one_example, 0)
    finish(n_steps * AT_ONCE, examples - 1)

    def across(r, carry):
        def here(i):
            start = PAD + i * block_rows + r * SUBLANES
            return pl.ds(pl.multiple_of(start, SUBLANES), SUBLANES)

        for b in range(bands):
            tiles = butterfly([t_ref[here(b * n_cols + q), :] for q in range(n_cols)])
            if b % 2 == 0:
                for q in range(n_cols):
                    t_ref[here(b * n_cols + q), :] = tiles[q]
            else:
                for q in range(n_cols):
                    low = t_ref[here((b - 1) * n_cols + q), :]
                    t_ref[here((b - 1) * n_cols + q), :] = low + tiles[q]
                    t_ref[here(b * n_cols + q), :] = low - tiles[q]
        return carry

    lax.fori_loop(0, block_rows // SUBLANES, across, 0)

    idx_copy.wait()
    lane = iota((SUBLANES, LANES), 1)
    spot = iota((SUBLANES, LANES), 0) // examples
    n_groups = n_kept // LANES // per_vreg
    half = n_groups // 2

    def one_group(group, out_ref, at, flip_ref):
        found = jnp.zeros((SUBLANES, LANES), jnp.float32)
        for u in range(LANES):
            term = None
            for p in range(per_vreg):
                tile = t_ref[pl.ds(idx_smem[group * per_vreg + p, u], SUBLANES), :]
                tile = tile * flip_ref[pl.ds(p * LANES + u, SUBLANES, stride=0), :]
                term = tile if p == 0 else jnp.where(spot == p, tile, term)
            total = jnp.sum(term, axis=1, keepdims=True)
            found = jnp.where(lane == u, total, found)
        for p in range(per_vreg):
            top = cols_ref[pl.ds(group * per_vreg + p, 1), :] // width // rows
            factor = (1 - 2 * parity(top & me)).astype(jnp.float32) * scale
            there = pl.ds(aligned(at * per_vreg + p, LANES), LANES)
            out_ref[:, there] = found[p * examples : (p + 1) * examples] * factor

    def sample(out_ref, base):
        def body(i, carry):
            group = base + 2 * i
            flips(group + 1, flip_odd)
            one_group(group, out_ref, 2 * i, flip_even)
            flips(lax.rem(group + 2, n_groups), flip_even)
            one_group(group + 1, out_ref, 2 * i + 1, flip_odd)
            return carry

        lax.fori_loop(0, half // 2, body, 0)

    theirs = (1 - me % 2) * half
    flips(theirs, flip_even)
    sample(other_ref, theirs)
    sample(mine_ref, me % 2 * half)


def sketch(x_acts, delta, pattern, sign_rows, col_signs, cols):
    examples, tokens, width = x_acts.shape
    rows = delta.shape[2]
    n_kept = cols.shape[0]
    bands = max(rows // BLK, 1)
    band = rows // bands
    n_blocks = bands * width // LANES
    per_vreg = SUBLANES // examples
    hbm = pl.BlockSpec(memory_space=pltpu.HBM)
    vmem = pl.BlockSpec(memory_space=pltpu.VMEM)
    scale = 1.0 / (tokens * math.sqrt(n_kept))
    part = jax.ShapeDtypeStruct((examples, n_kept // 2), jnp.float32)
    return pl.pallas_call(
        functools.partial(sketch_kernel, scale),
        out_shape=(part, part),
        in_specs=[hbm] * 6,
        out_specs=(vmem, vmem),
        scratch_shapes=[
            pltpu.SMEM(pattern.shape, jnp.int32),
            pltpu.VMEM((n_kept // LANES, LANES), jnp.int32),
            pltpu.VMEM(sign_rows.shape, jnp.int32),
            pltpu.VMEM((width // LANES, LANES), jnp.int32),
            pltpu.SemaphoreType.DMA((4,)),
            pltpu.VMEM((2, tokens, width), jnp.bfloat16),
            pltpu.VMEM((examples, tokens, rows), jnp.bfloat16),
            pltpu.VMEM((examples * bands, band, tokens), jnp.bfloat16),
            pltpu.VMEM((band, band), jnp.bfloat16),
            pltpu.VMEM((per_vreg * LANES, LANES), jnp.float32),
            pltpu.VMEM((per_vreg * LANES, LANES), jnp.float32),
            pltpu.VMEM((n_kept // LANES, LANES), jnp.int32),
            pltpu.VMEM((band, AT_ONCE * LANES), jnp.bfloat16),
            pltpu.VMEM((PAD + (n_blocks + 1) * band * examples, LANES), jnp.float32),
            pltpu.SemaphoreType.DMA((2, PARTS)),
            pltpu.SemaphoreType.DMA,
            pltpu.SemaphoreType.DMA,
            pltpu.SMEM((n_kept // LANES, LANES), jnp.int32),
            pltpu.SMEM((n_blocks + GROUP * bands + 2 * AT_ONCE,), jnp.int32),
        ],
        compiler_params=pltpu.CompilerParams(vmem_limit_bytes=VMEM_LIMIT),
    )(
        *(
            pltpu.with_memory_space_constraint(value, pltpu.HBM)
            for value in (
                pattern, x_acts, delta, cols.reshape(-1, LANES), sign_rows,
                col_signs.reshape(-1, LANES),
            )
        )
    )


def per_device(x_acts, delta, pattern, row_signs, col_signs, cols):
    rows = delta.shape[2]
    feat = lax.axis_size("feat")
    me = lax.axis_index("feat")
    if rows % LANES == 0:
        sign_rows = row_signs.reshape(-1, LANES)
    else:
        sign_rows = lax.dynamic_slice_in_dim(row_signs, me * rows, rows, 0)[None]

    mine, other = sketch(x_acts, delta, pattern, sign_rows, col_signs, cols)

    bits = max(feat - 1, 0).bit_length()
    mine = mine + partner(other, "feat", 0)
    for bit in range(1, bits):
        mine = mine + partner(mine, "feat", bit)
    back = partner(mine, "feat", 0)
    low = me % 2 == 0
    return jnp.concatenate([jnp.where(low, mine, back), jnp.where(low, back, mine)], axis=1)


def solution(mesh):
    placed = (P("grp", None, None), P("grp", None, "feat"), P(), P(), P(), P())
    return jax.shard_map(
        per_device, mesh=mesh, in_specs=placed, out_specs=P("grp", None), check_vma=False
    )
```

profile of v0, /device:TPU:0, one launch (start us, length us, event | category | flops | bytes accessed | tf_op | source)
XLA Modules:
  0.0 58.4 jit_solution(18345125435291795246)
XLA Ops:
  0.0 34.1 %shard_map.64 = (f32[4,4096]{1,0:T(4,128)S(1)}, f32[4,4096]{1,0:T(4,128)S(1)}) custom-call(s32[32,32]{1,0:T(8,128)} %pattern_hbm.1, bf16[4,1024,4096]{2,1,0:T(8,128)(2,1)} %x_hbm.1, bf16[4,1024,256]{2,1,0:T(8,128)(2,1)} %d_hbm.1, s32[64,128]{1,0:T(8,128)} %bitcast.3, s32[32,128]{1,0:T(8,128)} %bitcast.4, s32[32,128]{1,0:T(8,128)} %bitcast.5), custom_call_target="tpu_custom_call" | custom-call | tf_op jit(solution)/shard_map/pallas_call | solution.py:276
  34.1 3.7 %collective-permute-start = (f32[4,4096]{1,0:T(4,128)S(1)}, f32[4,4096]{1,0:T(4,128)S(1)}, u32[]{:S(2)}, u32[]{:S(2)}) collective-permute-start(f32[4,4096]{1,0:T(4,128)S(1)} %get-tuple-element.8), channel_id=1, source_target_pairs={{0,1},{1,0},{2,3},{3,2},{4,5},{5,4},{6,7},{7,6},{8,9},{9,8},{10,11... | collective-permute-start | bytes 196616 | tf_op jit(solution)/shard_map/ppermute | solution.py:24
  37.8 0.9 %collective-permute-done = f32[4,4096]{1,0:T(4,128)S(1)} collective-permute-done((f32[4,4096]{1,0:T(4,128)S(1)}, f32[4,4096]{1,0:T(4,128)S(1)}, u32[]{:S(2)}, u32[]{:S(2)}) %collective-permute-start) | collective-permute-done | bytes 65568 | tf_op jit(solution)/shard_map/ppermute | solution.py:24
  38.7 0.1 collective-permute-start.1
  38.8 4.3 %collective-permute-done.1 = f32[4,4096]{1,0:T(4,128)S(1)} collective-permute-done((f32[4,4096]{1,0:T(4,128)S(1)}, f32[4,4096]{1,0:T(4,128)S(1)}, u32[]{:S(2)}, u32[]{:S(2)}) %collective-permute-start.1) | collective-permute-done | bytes 65568 | tf_op jit(solution)/shard_map/ppermute | solution.py:24
  43.2 5.6 %collective-permute-start.2 = (f32[4,4096]{1,0:T(4,128)S(1)}, f32[4,4096]{1,0:T(4,128)S(1)}, u32[]{:S(2)}, u32[]{:S(2)}) collective-permute-start(f32[4,4096]{1,0:T(4,128)S(1)} %add.18), channel_id=1, source_target_pairs={{0,4},{1,5},{2,6},{3,7},{4,0},{5,1},{6,2},{7,3},{8,12},{9,13},{10,... | collective-permute-start | bytes 196616 | tf_op jit(solution)/shard_map/ppermute | solution.py:24
  48.8 2.2 %collective-permute-done.2 = f32[4,4096]{1,0:T(4,128)S(1)} collective-permute-done((f32[4,4096]{1,0:T(4,128)S(1)}, f32[4,4096]{1,0:T(4,128)S(1)}, u32[]{:S(2)}, u32[]{:S(2)}) %collective-permute-start.2) | collective-permute-done | bytes 65568 | tf_op jit(solution)/shard_map/ppermute | solution.py:24
  51.0 3.0 %collective-permute-start.3 = (f32[4,4096]{1,0:T(4,128)S(1)}, f32[4,4096]{1,0:T(4,128)S(1)}, u32[]{:S(2)}, u32[]{:S(2)}) collective-permute-start(f32[4,4096]{1,0:T(4,128)S(1)} %add.19), channel_id=1, source_target_pairs={{0,8},{1,9},{2,10},{3,11},{4,12},{5,13},{6,14},{7,15},{8,0},{9,1},... | collective-permute-start | bytes 196616 | tf_op jit(solution)/shard_map/ppermute | solution.py:24
  54.1 2.2 %collective-permute-done.3 = f32[4,4096]{1,0:T(4,128)S(1)} collective-permute-done((f32[4,4096]{1,0:T(4,128)S(1)}, f32[4,4096]{1,0:T(4,128)S(1)}, u32[]{:S(2)}, u32[]{:S(2)}) %collective-permute-start.3) | collective-permute-done | bytes 65568 | tf_op jit(solution)/shard_map/ppermute | solution.py:24
  56.4 0.1 collective-permute-start.4
  56.4 1.2 %collective-permute-done.4 = f32[4,4096]{1,0:T(4,128)S(1)} collective-permute-done((f32[4,4096]{1,0:T(4,128)S(1)}, f32[4,4096]{1,0:T(4,128)S(1)}, u32[]{:S(2)}, u32[]{:S(2)}) %collective-permute-start.4) | collective-permute-done | bytes 65568 | tf_op jit(solution)/shard_map/ppermute | solution.py:24
  57.7 0.7 %pad_maximum_fusion = f32[4,8192]{1,0:T(4,128)} fusion(f32[4,4096]{1,0:T(4,128)S(1)} %get-tuple-element.10, f32[4,4096]{1,0:T(4,128)S(1)} %get-tuple-element.9), kind=kLoop, calls=%fused_computation | loop fusion | flops 32768 | bytes 262144 | tf_op jit(solution)/shard_map/concatenate | solution.py:331
  (5 shorter events, 0.1 us)
Async XLA Ops:
  34.1 4.6 %collective-permute-start = (f32[4,4096]{1,0:T(4,128)S(1)}, f32[4,4096]{1,0:T(4,128)S(1)}, u32[]{:S(2)}, u32[]{:S(2)}) collective-permute-start(f32[4,4096]{1,0:T(4,128)S(1)} %get-tuple-element.8), channel_id=1, source_target_pairs={{0,1},{1,0},{2,3},{3,2},{4,5},{5,4},{6,7},{7,6},{8,9},{9,8},{10,11... | collective-permute-start | bytes 196616 | tf_op jit(solution)/shard_map/ppermute | solution.py:24
  38.7 4.4 %collective-permute-start.1 = (f32[4,4096]{1,0:T(4,128)S(1)}, f32[4,4096]{1,0:T(4,128)S(1)}, u32[]{:S(2)}, u32[]{:S(2)}) collective-permute-start(f32[4,4096]{1,0:T(4,128)S(1)} %add.17), channel_id=1, source_target_pairs={{0,2},{1,3},{2,0},{3,1},{4,6},{5,7},{6,4},{7,5},{8,10},{9,11},{10,... | collective-permute-start | bytes 196616 | tf_op jit(solution)/shard_map/ppermute | solution.py:24
  43.2 7.8 %collective-permute-start.2 = (f32[4,4096]{1,0:T(4,128)S(1)}, f32[4,4096]{1,0:T(4,128)S(1)}, u32[]{:S(2)}, u32[]{:S(2)}) collective-permute-start(f32[4,4096]{1,0:T(4,128)S(1)} %add.18), channel_id=1, source_target_pairs={{0,4},{1,5},{2,6},{3,7},{4,0},{5,1},{6,2},{7,3},{8,12},{9,13},{10,... | collective-permute-start | bytes 196616 | tf_op jit(solution)/shard_map/ppermute | solution.py:24
  51.0 5.3 %collective-permute-start.3 = (f32[4,4096]{1,0:T(4,128)S(1)}, f32[4,4096]{1,0:T(4,128)S(1)}, u32[]{:S(2)}, u32[]{:S(2)}) collective-permute-start(f32[4,4096]{1,0:T(4,128)S(1)} %add.19), channel_id=1, source_target_pairs={{0,8},{1,9},{2,10},{3,11},{4,12},{5,13},{6,14},{7,15},{8,0},{9,1},... | collective-permute-start | bytes 196616 | tf_op jit(solution)/shard_map/ppermute | solution.py:24
  56.4 1.3 %collective-permute-start.4 = (f32[4,4096]{1,0:T(4,128)S(1)}, f32[4,4096]{1,0:T(4,128)S(1)}, u32[]{:S(2)}, u32[]{:S(2)}) collective-permute-start(f32[4,4096]{1,0:T(4,128)S(1)} %add.20), channel_id=1, source_target_pairs={{0,1},{1,0},{2,3},{3,2},{4,5},{5,4},{6,7},{7,6},{8,9},{9,8},{10,11... | collective-permute-start | bytes 196616 | tf_op jit(solution)/shard_map/ppermute | solution.py:24
where the time goes:
time: 59 us; the launch traced here: 58.4 us
  Pallas kernels  34.1 us (58%)
  starting transfers between devices  12.5 us (21%)
  waiting for transfers between devices  11 us (19%)
  other arithmetic  0.78 us (1%)
    pallas_call x1, Pallas kernels, sketch(): pl.pallas_call(functools.partial(sketch_kernel, scale), out_shape=(part,...  34.1 us
    ppermute x5, starting transfers between devices, partner(): return lax.ppermute(value, axis, pairs)  12.5 us
    ppermute x5, waiting for transfers between devices, partner(): return lax.ppermute(value, axis, pairs)  11 us
  transfers between devices with their start and end apart: 5, of which 5 were waited for; matrix products, arithmetic and copies ran while one was open for 0% of the time, Pallas kernels for 0%

commit v1 on v0

--- a/solution.py
+++ b/solution.py
@@ -13,7 +13,6 @@
 SUBLANES = 8
 AT_ONCE = 8
 GROUP = 4
-PARTS = 4
 PAD = 8
 VMEM_LIMIT = 44 * 2**20
 
@@ -63,14 +62,28 @@
     n_kept = cols_ref.shape[0] * LANES
     per_vreg = SUBLANES // examples
     me = lax.axis_index("feat")
-    step = tokens // PARTS
-
-    def x_copy(example, part):
-        where = pl.ds(part * step, step)
+    first = me * rows // BLK
+
+    def x_copy(example, q):
         slot = example % 2
+        lanes = pl.ds(aligned(q, LANES), LANES)
         return pltpu.make_async_copy(
-            x_hbm.at[example, where], x_ref.at[slot, where], x_sem.at[slot, part]
+            x_hbm.at[example, :, lanes], x_ref.at[slot, q], x_sem.at[slot, q]
         )
+
+    def each_used(act):
+        def body(q, carry):
+            used = pattern[first, q]
+            for b in range(1, bands):
+                used = used | pattern[first + b, q]
+
+            @pl.when(used != 0)
+            def _():
+                act(q)
+
+            return carry
+
+        lax.fori_loop(0, n_cols, body, 0)
 
     small = [
         pltpu.make_async_copy(source, target, small_sem.at[i])
@@ -87,8 +100,8 @@
         copy.start()
     d_copy = pltpu.make_async_copy(d_hbm, d_ref, d_sem)
     d_copy.start()
-    for part in range(PARTS):
-        x_copy(0, part).start()
+    for q in range(n_cols):
+        x_copy(0, q).start()
 
     had_ref[...] = (1 - 2 * parity(iota((band, band), 0) & iota((band, band), 1))).astype(
         jnp.bfloat16
@@ -118,7 +131,6 @@
         odd = (shared.astype(jnp.int32) & 1).astype(jnp.float32)
         flip_ref[...] = 1.0 - 2.0 * odd
 
-    first = me * rows // BLK
 
     count = AT_ONCE
     for b in range(bands):
@@ -169,22 +181,24 @@
             t_ref[pl.ds(start, band, stride=examples), :] = sums[:, i * LANES : (i + 1) * LANES]
 
     def one_example(example, carry):
-        for part in range(PARTS):
-            x_copy(example, part).wait()
+        @pl.when(example == 0)
+        def _():
+            for q in range(n_cols):
+                x_copy(0, q).wait()
+
+        @pl.when(example > 0)
+        def _():
+            each_used(lambda q: x_copy(example, q).wait())
 
         @pl.when(example + 1 < examples)
         def _():
-            for part in range(PARTS):
-                x_copy(example + 1, part).start()
-
+            each_used(lambda q: x_copy(example + 1, q).start())
 
         def some_blocks(s, carry):
             finish(s * AT_ONCE, jnp.where(s == 0, jnp.maximum(example - 1, 0), example))
             for g in range(AT_ONCE // GROUP):
                 ids = [listed[(s + 1) * AT_ONCE + g * GROUP + k] for k in range(GROUP)]
-                acts = [
-                    x_ref[example % 2, :, pl.ds(aligned(i % n_cols, LANES), LANES)] for i in ids
-                ]
+                acts = [x_ref[example % 2, i % n_cols] for i in ids]
                 flip = [signs_ref[pl.ds(i % n_cols, 1), :] for i in ids]
                 grad = jnp.dot(
                     dt_ref[example * bands + ids[0] // n_cols % bands],
@@ -284,7 +298,7 @@
             pltpu.VMEM(sign_rows.shape, jnp.int32),
             pltpu.VMEM((width // LANES, LANES), jnp.int32),
             pltpu.SemaphoreType.DMA((4,)),
-            pltpu.VMEM((2, tokens, width), jnp.bfloat16),
+            pltpu.VMEM((2, width // LANES, tokens, LANES), jnp.bfloat16),
             pltpu.VMEM((examples, tokens, rows), jnp.bfloat16),
             pltpu.VMEM((examples * bands, band, tokens), jnp.bfloat16),
             pltpu.VMEM((band, band), jnp.bfloat16),
@@ -293,7 +307,7 @@
             pltpu.VMEM((n_kept // LANES, LANES), jnp.int32),
             pltpu.VMEM((band, AT_ONCE * LANES), jnp.bfloat16),
             pltpu.VMEM((PAD + (n_blocks + 1) * band * examples, LANES), jnp.float32),
-            pltpu.SemaphoreType.DMA((2, PARTS)),
+            pltpu.SemaphoreType.DMA((2, width // LANES)),
             pltpu.SemaphoreType.DMA,
             pltpu.SemaphoreType.DMA,
             pltpu.SMEM((n_kept // LANES, LANES), jnp.int32),

time: 59 us -> 56 us (0.949)
  starting transfers between devices: 12.5 us -> 9.4 us
  Pallas kernels: 34.1 us -> 35.4 us
  waiting for transfers between devices: 11 us -> 10.3 us
    ppermute x5, starting transfers between devices: 12.5 us -> 9.4 us  [partner(): return lax.ppermute(value, axis, pairs)]
    pallas_call x1, Pallas kernels: 34.1 us -> 35.4 us  [sketch(): pl.pallas_call(functools.partial(sketch_kernel, scale), out_shape=(part,...]
    ppermute x5, waiting for transfers between devices: 11 us -> 10.3 us  [partner(): return lax.ppermute(value, axis, pairs)]
where the time goes in v1:
time: 56 us; the launch traced here: 55.9 us
  Pallas kernels  35.4 us (63%)
  waiting for transfers between devices  10.3 us (18%)
  starting transfers between devices  9.4 us (17%)
  other arithmetic  0.78 us (1%)
    pallas_call x1, Pallas kernels, sketch(): pl.pallas_call(functools.partial(sketch_kernel, scale), out_shape=(part,...  35.4 us
    ppermute x5, waiting for transfers between devices, partner(): return lax.ppermute(value, axis, pairs)  10.3 us
    ppermute x5, starting transfers between devices, partner(): return lax.ppermute(value, axis, pairs)  9.4 us
  transfers between devices with their start and end apart: 5, of which 5 were waited for; matrix products, arithmetic and copies ran while one was open for 0% of the time, Pallas kernels for 0%

profile of v1, /device:TPU:0, one launch (start us, length us, event | category | flops | bytes accessed | tf_op | source)
XLA Modules:
  0.0 55.9 jit_solution(3925812650640460293)
XLA Ops:
  0.0 35.4 %shard_map.64 = (f32[4,4096]{1,0:T(4,128)S(1)}, f32[4,4096]{1,0:T(4,128)S(1)}) custom-call(s32[32,32]{1,0:T(8,128)} %pattern_hbm.1, bf16[4,1024,4096]{2,1,0:T(8,128)(2,1)} %x_hbm.1, bf16[4,1024,256]{2,1,0:T(8,128)(2,1)} %d_hbm.1, s32[64,128]{1,0:T(8,128)} %bitcast.3, s32[32,128]{1,0:T(8,128)} %bitcast.4, s32[32,128]{1,0:T(8,128)} %bitcast.5), custom_call_target="tpu_custom_call" | custom-call | tf_op jit(solution)/shard_map/pallas_call | solution.py:290
  35.4 0.6 %collective-permute-start = (f32[4,4096]{1,0:T(4,128)S(1)}, f32[4,4096]{1,0:T(4,128)S(1)}, u32[]{:S(2)}, u32[]{:S(2)}) collective-permute-start(f32[4,4096]{1,0:T(4,128)S(1)} %get-tuple-element.8), channel_id=1, source_target_pairs={{0,1},{1,0},{2,3},{3,2},{4,5},{5,4},{6,7},{7,6},{8,9},{9,8},{10,11... | collective-permute-start | bytes 196616 | tf_op jit(solution)/shard_map/ppermute | solution.py:23
  36.0 0.9 %collective-permute-done = f32[4,4096]{1,0:T(4,128)S(1)} collective-permute-done((f32[4,4096]{1,0:T(4,128)S(1)}, f32[4,4096]{1,0:T(4,128)S(1)}, u32[]{:S(2)}, u32[]{:S(2)}) %collective-permute-start) | collective-permute-done | bytes 65568 | tf_op jit(solution)/shard_map/ppermute | solution.py:23
  36.9 5.0 %collective-permute-start.1 = (f32[4,4096]{1,0:T(4,128)S(1)}, f32[4,4096]{1,0:T(4,128)S(1)}, u32[]{:S(2)}, u32[]{:S(2)}) collective-permute-start(f32[4,4096]{1,0:T(4,128)S(1)} %add.17), channel_id=1, source_target_pairs={{0,2},{1,3},{2,0},{3,1},{4,6},{5,7},{6,4},{7,5},{8,10},{9,11},{10,... | collective-permute-start | bytes 196616 | tf_op jit(solution)/shard_map/ppermute | solution.py:23
  41.9 2.4 %collective-permute-done.1 = f32[4,4096]{1,0:T(4,128)S(1)} collective-permute-done((f32[4,4096]{1,0:T(4,128)S(1)}, f32[4,4096]{1,0:T(4,128)S(1)}, u32[]{:S(2)}, u32[]{:S(2)}) %collective-permute-start.1) | collective-permute-done | bytes 65568 | tf_op jit(solution)/shard_map/ppermute | solution.py:23
  44.3 1.7 %collective-permute-start.2 = (f32[4,4096]{1,0:T(4,128)S(1)}, f32[4,4096]{1,0:T(4,128)S(1)}, u32[]{:S(2)}, u32[]{:S(2)}) collective-permute-start(f32[4,4096]{1,0:T(4,128)S(1)} %add.18), channel_id=1, source_target_pairs={{0,4},{1,5},{2,6},{3,7},{4,0},{5,1},{6,2},{7,3},{8,12},{9,13},{10,... | collective-permute-start | bytes 196616 | tf_op jit(solution)/shard_map/ppermute | solution.py:23
  46.0 2.7 %collective-permute-done.2 = f32[4,4096]{1,0:T(4,128)S(1)} collective-permute-done((f32[4,4096]{1,0:T(4,128)S(1)}, f32[4,4096]{1,0:T(4,128)S(1)}, u32[]{:S(2)}, u32[]{:S(2)}) %collective-permute-start.2) | collective-permute-done | bytes 65568 | tf_op jit(solution)/shard_map/ppermute | solution.py:23
  48.7 2.1 %collective-permute-start.3 = (f32[4,4096]{1,0:T(4,128)S(1)}, f32[4,4096]{1,0:T(4,128)S(1)}, u32[]{:S(2)}, u32[]{:S(2)}) collective-permute-start(f32[4,4096]{1,0:T(4,128)S(1)} %add.19), channel_id=1, source_target_pairs={{0,8},{1,9},{2,10},{3,11},{4,12},{5,13},{6,14},{7,15},{8,0},{9,1},... | collective-permute-start | bytes 196616 | tf_op jit(solution)/shard_map/ppermute | solution.py:23
  50.8 3.1 %collective-permute-done.3 = f32[4,4096]{1,0:T(4,128)S(1)} collective-permute-done((f32[4,4096]{1,0:T(4,128)S(1)}, f32[4,4096]{1,0:T(4,128)S(1)}, u32[]{:S(2)}, u32[]{:S(2)}) %collective-permute-start.3) | collective-permute-done | bytes 65568 | tf_op jit(solution)/shard_map/ppermute | solution.py:23
  53.9 0.1 collective-permute-start.4
  54.0 1.2 %collective-permute-done.4 = f32[4,4096]{1,0:T(4,128)S(1)} collective-permute-done((f32[4,4096]{1,0:T(4,128)S(1)}, f32[4,4096]{1,0:T(4,128)S(1)}, u32[]{:S(2)}, u32[]{:S(2)}) %collective-permute-start.4) | collective-permute-done | bytes 65568 | tf_op jit(solution)/shard_map/ppermute | solution.py:23
  55.3 0.7 %pad_maximum_fusion = f32[4,8192]{1,0:T(4,128)} fusion(f32[4,4096]{1,0:T(4,128)S(1)} %get-tuple-element.10, f32[4,4096]{1,0:T(4,128)S(1)} %get-tuple-element.9), kind=kLoop, calls=%fused_computation | loop fusion | flops 32768 | bytes 262144 | tf_op jit(solution)/shard_map/concatenate | solution.py:345
  (5 shorter events, 0.1 us)
Async XLA Ops:
  35.4 1.5 %collective-permute-start = (f32[4,4096]{1,0:T(4,128)S(1)}, f32[4,4096]{1,0:T(4,128)S(1)}, u32[]{:S(2)}, u32[]{:S(2)}) collective-permute-start(f32[4,4096]{1,0:T(4,128)S(1)} %get-tuple-element.8), channel_id=1, source_target_pairs={{0,1},{1,0},{2,3},{3,2},{4,5},{5,4},{6,7},{7,6},{8,9},{9,8},{10,11... | collective-permute-start | bytes 196616 | tf_op jit(solution)/shard_map/ppermute | solution.py:23
  36.9 7.4 %collective-permute-start.1 = (f32[4,4096]{1,0:T(4,128)S(1)}, f32[4,4096]{1,0:T(4,128)S(1)}, u32[]{:S(2)}, u32[]{:S(2)}) collective-permute-start(f32[4,4096]{1,0:T(4,128)S(1)} %add.17), channel_id=1, source_target_pairs={{0,2},{1,3},{2,0},{3,1},{4,6},{5,7},{6,4},{7,5},{8,10},{9,11},{10,... | collective-permute-start | bytes 196616 | tf_op jit(solution)/shard_map/ppermute | solution.py:23
  44.3 4.3 %collective-permute-start.2 = (f32[4,4096]{1,0:T(4,128)S(1)}, f32[4,4096]{1,0:T(4,128)S(1)}, u32[]{:S(2)}, u32[]{:S(2)}) collective-permute-start(f32[4,4096]{1,0:T(4,128)S(1)} %add.18), channel_id=1, source_target_pairs={{0,4},{1,5},{2,6},{3,7},{4,0},{5,1},{6,2},{7,3},{8,12},{9,13},{10,... | collective-permute-start | bytes 196616 | tf_op jit(solution)/shard_map/ppermute | solution.py:23
  48.7 5.2 %collective-permute-start.3 = (f32[4,4096]{1,0:T(4,128)S(1)}, f32[4,4096]{1,0:T(4,128)S(1)}, u32[]{:S(2)}, u32[]{:S(2)}) collective-permute-start(f32[4,4096]{1,0:T(4,128)S(1)} %add.19), channel_id=1, source_target_pairs={{0,8},{1,9},{2,10},{3,11},{4,12},{5,13},{6,14},{7,15},{8,0},{9,1},... | collective-permute-start | bytes 196616 | tf_op jit(solution)/shard_map/ppermute | solution.py:23
  53.9 1.3 %collective-permute-start.4 = (f32[4,4096]{1,0:T(4,128)S(1)}, f32[4,4096]{1,0:T(4,128)S(1)}, u32[]{:S(2)}, u32[]{:S(2)}) collective-permute-start(f32[4,4096]{1,0:T(4,128)S(1)} %add.20), channel_id=1, source_target_pairs={{0,1},{1,0},{2,3},{3,2},{4,5},{5,4},{6,7},{7,6},{8,9},{9,8},{10,11... | collective-permute-start | bytes 196616 | tf_op jit(solution)/shard_map/ppermute | solution.py:23

commit v2 on v1

--- a/solution.py
+++ b/solution.py
@@ -13,6 +13,7 @@
 SUBLANES = 8
 AT_ONCE = 8
 GROUP = 4
+RADIX = 16
 PAD = 8
 VMEM_LIMIT = 44 * 2**20
 
@@ -50,7 +51,7 @@
 
 def sketch_kernel(
     scale, pattern_hbm, x_hbm, d_hbm, cols_hbm, rows_hbm, signs_hbm, mine_ref, other_ref,
-    pattern, cols_ref, rows_ref, signs_ref, small_sem, x_ref, d_ref, dt_ref, had_ref, flip_even, flip_odd, idx_ref, signed_ref, t_ref, x_sem, d_sem, idx_sem, idx_smem, listed,
+    pattern, cols_ref, rows_ref, signs_ref, small_sem, x_ref, d_ref, dt_ref, had_ref, flip_even, flip_odd, idx_ref, signed_ref, t_ref, x_sem, d_sem, idx_sem, idx_smem, listed, left_out,
 ):
     examples, tokens, width = x_hbm.shape
     rows = d_hbm.shape[2]
@@ -71,7 +72,7 @@
             x_hbm.at[example, :, lanes], x_ref.at[slot, q], x_sem.at[slot, q]
         )
 
-    def each_used(act):
+    def each_used(act, begin, end):
         def body(q, carry):
             used = pattern[first, q]
             for b in range(1, bands):
@@ -83,8 +84,14 @@
 
             return carry
 
-        lax.fori_loop(0, n_cols, body, 0)
-
+        lax.fori_loop(begin, end, body, 0)
+
+    def start_used(example, begin, end):
+        @pl.when(example < examples)
+        def _():
+            each_used(lambda q: x_copy(example, q).start(), begin, end)
+
+    ahead = n_cols // 2
     small = [
         pltpu.make_async_copy(source, target, small_sem.at[i])
         for i, (source, target) in enumerate(
@@ -148,18 +155,20 @@
 
     idx_copy = pltpu.make_async_copy(idx_ref, idx_smem, idx_sem)
     idx_copy.start()
-
-    for b in range(bands):
-        def clear(q, carry):
-            @pl.when(pattern[first + b, q] == 0)
-            def _():
-                start = PAD + (b * n_cols + q) * block_rows
-                here = pl.ds(pl.multiple_of(start, SUBLANES), block_rows)
-                t_ref[here, :] = jnp.zeros((block_rows, LANES), jnp.float32)
-
-            return carry
-
-        lax.fori_loop(0, n_cols, clear, 0)
+    start_used(1, 0, ahead)
+
+    spare = 0
+    for i in range(n_blocks):
+        left_out[spare] = i
+        spare = spare + 1 - pattern[first + i // n_cols, i % n_cols]
+
+    def clear(i, carry):
+        start = PAD + left_out[i] * block_rows
+        here = pl.ds(pl.multiple_of(start, SUBLANES), block_rows)
+        t_ref[here, :] = jnp.zeros((block_rows, LANES), jnp.float32)
+        return carry
+
+    lax.fori_loop(0, spare, clear, 0)
 
     if rows % LANES == 0:
         row_flip = jnp.concatenate(
@@ -188,11 +197,10 @@
 
         @pl.when(example > 0)
         def _():
-            each_used(lambda q: x_copy(example, q).wait())
-
-        @pl.when(example + 1 < examples)
-        def _():
-            each_used(lambda q: x_copy(example + 1, q).start())
+            start_used(example + 1, 0, ahead)
+            each_used(lambda q: x_copy(example, q).wait(), 0, n_cols)
+
+        start_used(example + 1, ahead, n_cols)
 
         def some_blocks(s, carry):
             finish(s * AT_ONCE, jnp.where(s == 0, jnp.maximum(example - 1, 0), example))
@@ -222,16 +230,16 @@
             start = PAD + i * block_rows + r * SUBLANES
             return pl.ds(pl.multiple_of(start, SUBLANES), SUBLANES)
 
-        for b in range(bands):
-            tiles = butterfly([t_ref[here(b * n_cols + q), :] for q in range(n_cols)])
-            if b % 2 == 0:
-                for q in range(n_cols):
-                    t_ref[here(b * n_cols + q), :] = tiles[q]
-            else:
-                for q in range(n_cols):
-                    low = t_ref[here((b - 1) * n_cols + q), :]
-                    t_ref[here((b - 1) * n_cols + q), :] = low + tiles[q]
-                    t_ref[here(b * n_cols + q), :] = low - tiles[q]
+        done = 1
+        while done < n_blocks:
+            radix = min(RADIX, n_blocks // done)
+            for lead in range(0, n_blocks, done * radix):
+                for low in range(done):
+                    ids = [lead + low + k * done for k in range(radix)]
+                    tiles = butterfly([t_ref[here(i), :] for i in ids])
+                    for i, tile in zip(ids, tiles):
+                        t_ref[here(i), :] = tile
+            done *= radix
         return carry
 
     lax.fori_loop(0, block_rows // SUBLANES, across, 0)
@@ -312,6 +320,7 @@
             pltpu.SemaphoreType.DMA,
             pltpu.SMEM((n_kept // LANES, LANES), jnp.int32),
             pltpu.SMEM((n_blocks + GROUP * bands + 2 * AT_ONCE,), jnp.int32),
+            pltpu.SMEM((n_blocks,), jnp.int32),
         ],
         compiler_params=pltpu.CompilerParams(vmem_limit_bytes=VMEM_LIMIT),
     )(

time: 56 us -> 52.6 us (0.939)
  starting transfers between devices: 9.4 us -> 7.38 us
  Pallas kernels: 35.4 us -> 34.1 us
    ppermute x5, starting transfers between devices: 9.4 us -> 7.38 us  [partner(): return lax.ppermute(value, axis, pairs)]
    pallas_call x1, Pallas kernels: 35.4 us -> 34.1 us  [sketch(): pl.pallas_call(functools.partial(sketch_kernel, scale), out_shape=(part,...]
where the time goes in v2:
time: 52.6 us; the launch traced here: 52.5 us
  Pallas kernels  34.1 us (65%)
  waiting for transfers between devices  10.3 us (20%)
  starting transfers between devices  7.38 us (14%)
  other arithmetic  0.78 us (1%)
    pallas_call x1, Pallas kernels, sketch(): pl.pallas_call(functools.partial(sketch_kernel, scale), out_shape=(part,...  34.1 us
    ppermute x5, waiting for transfers between devices, partner(): return lax.ppermute(value, axis, pairs)  10.3 us
    ppermute x5, starting transfers between devices, partner(): return lax.ppermute(value, axis, pairs)  7.38 us
  transfers between devices with their start and end apart: 5, of which 5 were waited for; matrix products, arithmetic and copies ran while one was open for 0% of the time, Pallas kernels for 0%

profile of v2, /device:TPU:0, one launch (start us, length us, event | category | flops | bytes accessed | tf_op | source)
XLA Modules:
  0.0 52.5 jit_solution(2275347348044441260)
XLA Ops:
  0.0 34.1 %shard_map.64 = (f32[4,4096]{1,0:T(4,128)S(1)}, f32[4,4096]{1,0:T(4,128)S(1)}) custom-call(s32[32,32]{1,0:T(8,128)} %pattern_hbm.1, bf16[4,1024,4096]{2,1,0:T(8,128)(2,1)} %x_hbm.1, bf16[4,1024,256]{2,1,0:T(8,128)(2,1)} %d_hbm.1, s32[64,128]{1,0:T(8,128)} %bitcast.3, s32[32,128]{1,0:T(8,128)} %bitcast.4, s32[32,128]{1,0:T(8,128)} %bitcast.5), custom_call_target="tpu_custom_call" | custom-call | tf_op jit(solution)/shard_map/pallas_call | solution.py:298
  34.1 0.6 %collective-permute-start = (f32[4,4096]{1,0:T(4,128)S(1)}, f32[4,4096]{1,0:T(4,128)S(1)}, u32[]{:S(2)}, u32[]{:S(2)}) collective-permute-start(f32[4,4096]{1,0:T(4,128)S(1)} %get-tuple-element.8), channel_id=1, source_target_pairs={{0,1},{1,0},{2,3},{3,2},{4,5},{5,4},{6,7},{7,6},{8,9},{9,8},{10,11... | collective-permute-start | bytes 196616 | tf_op jit(solution)/shard_map/ppermute | solution.py:24
  34.6 0.9 %collective-permute-done = f32[4,4096]{1,0:T(4,128)S(1)} collective-permute-done((f32[4,4096]{1,0:T(4,128)S(1)}, f32[4,4096]{1,0:T(4,128)S(1)}, u32[]{:S(2)}, u32[]{:S(2)}) %collective-permute-start) | collective-permute-done | bytes 65568 | tf_op jit(solution)/shard_map/ppermute | solution.py:24
  35.6 0.8 %collective-permute-start.1 = (f32[4,4096]{1,0:T(4,128)S(1)}, f32[4,4096]{1,0:T(4,128)S(1)}, u32[]{:S(2)}, u32[]{:S(2)}) collective-permute-start(f32[4,4096]{1,0:T(4,128)S(1)} %add.17), channel_id=1, source_target_pairs={{0,2},{1,3},{2,0},{3,1},{4,6},{5,7},{6,4},{7,5},{8,10},{9,11},{10,... | collective-permute-start | bytes 196616 | tf_op jit(solution)/shard_map/ppermute | solution.py:24
  36.3 3.7 %collective-permute-done.1 = f32[4,4096]{1,0:T(4,128)S(1)} collective-permute-done((f32[4,4096]{1,0:T(4,128)S(1)}, f32[4,4096]{1,0:T(4,128)S(1)}, u32[]{:S(2)}, u32[]{:S(2)}) %collective-permute-start.1) | collective-permute-done | bytes 65568 | tf_op jit(solution)/shard_map/ppermute | solution.py:24
  40.0 2.8 %collective-permute-start.2 = (f32[4,4096]{1,0:T(4,128)S(1)}, f32[4,4096]{1,0:T(4,128)S(1)}, u32[]{:S(2)}, u32[]{:S(2)}) collective-permute-start(f32[4,4096]{1,0:T(4,128)S(1)} %add.18), channel_id=1, source_target_pairs={{0,4},{1,5},{2,6},{3,7},{4,0},{5,1},{6,2},{7,3},{8,12},{9,13},{10,... | collective-permute-start | bytes 196616 | tf_op jit(solution)/shard_map/ppermute | solution.py:24
  42.8 2.2 %collective-permute-done.2 = f32[4,4096]{1,0:T(4,128)S(1)} collective-permute-done((f32[4,4096]{1,0:T(4,128)S(1)}, f32[4,4096]{1,0:T(4,128)S(1)}, u32[]{:S(2)}, u32[]{:S(2)}) %collective-permute-start.2) | collective-permute-done | bytes 65568 | tf_op jit(solution)/shard_map/ppermute | solution.py:24
  45.0 3.2 %collective-permute-start.3 = (f32[4,4096]{1,0:T(4,128)S(1)}, f32[4,4096]{1,0:T(4,128)S(1)}, u32[]{:S(2)}, u32[]{:S(2)}) collective-permute-start(f32[4,4096]{1,0:T(4,128)S(1)} %add.19), channel_id=1, source_target_pairs={{0,8},{1,9},{2,10},{3,11},{4,12},{5,13},{6,14},{7,15},{8,0},{9,1},... | collective-permute-start | bytes 196616 | tf_op jit(solution)/shard_map/ppermute | solution.py:24
  48.2 2.2 %collective-permute-done.3 = f32[4,4096]{1,0:T(4,128)S(1)} collective-permute-done((f32[4,4096]{1,0:T(4,128)S(1)}, f32[4,4096]{1,0:T(4,128)S(1)}, u32[]{:S(2)}, u32[]{:S(2)}) %collective-permute-start.3) | collective-permute-done | bytes 65568 | tf_op jit(solution)/shard_map/ppermute | solution.py:24
  50.5 0.1 collective-permute-start.4
  50.6 1.2 %collective-permute-done.4 = f32[4,4096]{1,0:T(4,128)S(1)} collective-permute-done((f32[4,4096]{1,0:T(4,128)S(1)}, f32[4,4096]{1,0:T(4,128)S(1)}, u32[]{:S(2)}, u32[]{:S(2)}) %collective-permute-start.4) | collective-permute-done | bytes 65568 | tf_op jit(solution)/shard_map/ppermute | solution.py:24
  51.9 0.7 %pad_maximum_fusion = f32[4,8192]{1,0:T(4,128)} fusion(f32[4,4096]{1,0:T(4,128)S(1)} %get-tuple-element.10, f32[4,4096]{1,0:T(4,128)S(1)} %get-tuple-element.9), kind=kLoop, calls=%fused_computation | loop fusion | flops 32768 | bytes 262144 | tf_op jit(solution)/shard_map/concatenate | solution.py:354
  (5 shorter events, 0.1 us)
Async XLA Ops:
  34.1 1.5 %collective-permute-start = (f32[4,4096]{1,0:T(4,128)S(1)}, f32[4,4096]{1,0:T(4,128)S(1)}, u32[]{:S(2)}, u32[]{:S(2)}) collective-permute-start(f32[4,4096]{1,0:T(4,128)S(1)} %get-tuple-element.8), channel_id=1, source_target_pairs={{0,1},{1,0},{2,3},{3,2},{4,5},{5,4},{6,7},{7,6},{8,9},{9,8},{10,11... | collective-permute-start | bytes 196616 | tf_op jit(solution)/shard_map/ppermute | solution.py:24
  35.6 4.4 %collective-permute-start.1 = (f32[4,4096]{1,0:T(4,128)S(1)}, f32[4,4096]{1,0:T(4,128)S(1)}, u32[]{:S(2)}, u32[]{:S(2)}) collective-permute-start(f32[4,4096]{1,0:T(4,128)S(1)} %add.17), channel_id=1, source_target_pairs={{0,2},{1,3},{2,0},{3,1},{4,6},{5,7},{6,4},{7,5},{8,10},{9,11},{10,... | collective-permute-start | bytes 196616 | tf_op jit(solution)/shard_map/ppermute | solution.py:24
  40.0 5.0 %collective-permute-start.2 = (f32[4,4096]{1,0:T(4,128)S(1)}, f32[4,4096]{1,0:T(4,128)S(1)}, u32[]{:S(2)}, u32[]{:S(2)}) collective-permute-start(f32[4,4096]{1,0:T(4,128)S(1)} %add.18), channel_id=1, source_target_pairs={{0,4},{1,5},{2,6},{3,7},{4,0},{5,1},{6,2},{7,3},{8,12},{9,13},{10,... | collective-permute-start | bytes 196616 | tf_op jit(solution)/shard_map/ppermute | solution.py:24
  45.0 5.5 %collective-permute-start.3 = (f32[4,4096]{1,0:T(4,128)S(1)}, f32[4,4096]{1,0:T(4,128)S(1)}, u32[]{:S(2)}, u32[]{:S(2)}) collective-permute-start(f32[4,4096]{1,0:T(4,128)S(1)} %add.19), channel_id=1, source_target_pairs={{0,8},{1,9},{2,10},{3,11},{4,12},{5,13},{6,14},{7,15},{8,0},{9,1},... | collective-permute-start | bytes 196616 | tf_op jit(solution)/shard_map/ppermute | solution.py:24
  50.5 1.3 %collective-permute-start.4 = (f32[4,4096]{1,0:T(4,128)S(1)}, f32[4,4096]{1,0:T(4,128)S(1)}, u32[]{:S(2)}, u32[]{:S(2)}) collective-permute-start(f32[4,4096]{1,0:T(4,128)S(1)} %add.20), channel_id=1, source_target_pairs={{0,1},{1,0},{2,3},{3,2},{4,5},{5,4},{6,7},{7,6},{8,9},{9,8},{10,11... | collective-permute-start | bytes 196616 | tf_op jit(solution)/shard_map/ppermute | solution.py:24
